TPU v7x, 32 devices: a whole 2x2x4 slice. The times are simulated.
32 devices in a mesh: depth: 16 (over z, y, x), samp: 2 (over core).
Axes of the slice: x: 2, y: 2, z: 4, core: 2. Of those that a mesh axis runs over, the one named last changes fastest.
Arguments:
- activations: bfloat16 [2, 16, 64, 16, 128], P('samp', 'depth'), may hold values from -6 to 6
- preact: bfloat16 [2, 16, 64, 16, 128], P('samp', 'depth'), may hold values from -6 to 6
- out_grad: bfloat16 [2, 16, 64, 16, 128], P('samp', 'depth'), may hold values from -6 to 6
- weights: bfloat16 [3, 3, 3, 128, 128], replicated, may hold values from -0.109375 to 0.109375
- master: float32 [442368], P(('depth', 'samp')), may hold values from -0.109375 to 0.109375
- moment: float32 [442368], P(('depth', 'samp')), may hold values from -4 to 4
- second: float32 [442368], P(('depth', 'samp')), may hold values from 0.1 to 1
Outputs:
- grad_input: bfloat16 [2, 16, 64, 16, 128], P('samp', 'depth')
- filter_grad: float32 [442368], P(('depth', 'samp'))
- new_moment: float32 [442368], P(('depth', 'samp'))
- new_second: float32 [442368], P(('depth', 'samp'))
- new_master: float32 [442368], P(('depth', 'samp'))
- new_weights: bfloat16 [3, 3, 3, 128, 128], replicated
All inputs are finite; a program needn't handle non-finite values.
Results may differ from a plain program's by a relative error of at most 0.001.
Values may be sent and summed in bfloat16 or wider, within the bound.
No kernel may reach another device: no remote copies, remote signals or barrier semaphores. Data moves between devices by JAX's collectives and lax.ppermute only.
A program may use at most 64 MiB of HBM per device.

v0:
```python
import jax
import jax.numpy as jnp
from jax import lax
from jax.sharding import PartitionSpec as P

first_fix = 1.0
second_fix = 0.63230457524


def padded(array, sides, width):
    for axis, dim in sides:
        peers, length = (lax.axis_size(axis), array.shape[dim])
        up = [(i, (i + 1) % peers) for i in range(peers - 1)]
        down = [(j, i) for i, j in up]
        last = lax.slice_in_dim(array, length - width, length, axis=dim)
        first = lax.slice_in_dim(array, 0, width, axis=dim)
        before = lax.ppermute(last, axis, up)
        after = lax.ppermute(first, axis, down)
        array = jnp.concatenate([before, array, after], axis=dim)
    return array


def contract_rows(left, right):
    return lax.dot_general(
        left, right, (((0,), (0,)), ((), ())), preferred_element_type=jnp.float32
    )


def local(activations, preact, out_grad, weights, master, moment, second):
    samples = activations.shape[0]
    planes = activations.shape[1]
    height = activations.shape[2]
    width = activations.shape[3]
    chans = activations.shape[4]
    count = samples * lax.axis_size("samp") * planes * lax.axis_size("depth") * height * width
    slope = jnp.where(preact > 0, jnp.float32(1.0), jnp.float32(0.01))
    cotangent = (out_grad.astype(jnp.float32) * slope).astype(jnp.bfloat16)
    side_pad = ((0, 0), (0, 0), (1, 1), (1, 1), (0, 0))
    extended = padded(cotangent, (("depth", 1),), 1)
    padded_cot = jnp.pad(extended, side_pad)
    flat_src = activations.reshape(-1, chans)
    result = jnp.zeros((samples * planes * height * width, chans), jnp.float32)
    terms = []
    for depth_tap in range(3):
        for row_tap in range(3):
            for col_tap in range(3):
                cot_part = padded_cot[
                    :,
                    2 - depth_tap : 2 - depth_tap + planes,
                    2 - row_tap : 2 - row_tap + height,
                    2 - col_tap : 2 - col_tap + width,
                ]
                cot_rows = cot_part.reshape(-1, chans)
                result = result + jnp.dot(
                    cot_rows,
                    weights[depth_tap, row_tap, col_tap].T,
                    preferred_element_type=jnp.float32,
                )
                terms.append(contract_rows(flat_src, cot_rows))
    grad_input = result.reshape(samples, planes, height, width, chans).astype(jnp.bfloat16)
    local_grad = jnp.stack(terms).reshape(-1) * jnp.float32(1.0 / count**0.5)
    filter_grad = lax.psum_scatter(local_grad, ("depth", "samp"), scatter_dimension=0, tiled=True)
    new_moment = 0.9 * moment + 0.1 * filter_grad
    new_second = 0.999 * second + 0.001 * filter_grad * filter_grad
    new_master = master - 0.01 * (new_moment / first_fix) / (
        jnp.sqrt(new_second / second_fix) + 1e-08
    )
    share = new_master.astype(jnp.bfloat16)
    whole = lax.all_gather(share, ("depth", "samp"), axis=0, tiled=True)
    new_weights = whole.reshape(3, 3, 3, chans, chans)
    return (grad_input, filter_grad, new_moment, new_second, new_master, new_weights)


def solution(mesh):
    return jax.shard_map(
        local,
        mesh=mesh,
        in_specs=(
            P("samp", "depth", None, None, None),
            P("samp", "depth", None, None, None),
            P("samp", "depth", None, None, None),
            P(),
            P(("depth", "samp")),
            P(("depth", "samp")),
            P(("depth", "samp")),
        ),
        out_specs=(
            P("samp", "depth", None, None, None),
            P(("depth", "samp")),
            P(("depth", "samp")),
            P(("depth", "samp")),
            P(("depth", "samp")),
            P(),
        ),
        check_vma=False,
    )
```

profile of v0, /device:TPU:0, one launch (start us, length us, event | category | flops | bytes accessed | tf_op | source)
XLA Modules:
  0.0 239.2 jit_solution(851903629191399208)
XLA Ops:
  7.2 1.2 multiply_convert_fusion
  8.4 1.3 collective-permute-start.1
  9.7 5.5 %collective-permute-start = (bf16[1,1,64,16,128]{4,2,3,1,0:T(8,128)(2,1)S(1)}, bf16[1,1,64,16,128]{4,2,3,1,0:T(8,128)(2,1)S(1)}, u32[]{:S(2)}, u32[]{:S(2)}) collective-permute-start(bf16[1,1,64,16,128]{4,2,3,1,0:T(8,128)(2,1)S(1)} %multiply_convert_fusion), channel_id=1, source_target_pairs={{0,2},{2,4},{4,6},{6,8},{8,10},{10,12},{12,14},{14,16},{16,18},{18... | collective-permute-start | bytes 786440 | tf_op jit(solution)/shard_map/ppermute | solution.py:17
  15.2 0.9 copy.171
  16.1 4.3 %collective-permute-done.1 = bf16[1,1,64,16,128]{4,2,3,1,0:T(8,128)(2,1)S(1)} collective-permute-done((bf16[1,1,64,16,128]{4,2,3,1,0:T(8,128)(2,1)S(1)}, bf16[1,1,64,16,128]{4,2,3,1,0:T(8,128)(2,1)S(1)}, u32[]{:S(2)}, u32[]{:S(2)}) %collective-permute-start.1) | collective-permute-done | bytes 262176 | tf_op jit(solution)/shard_map/ppermute | solution.py:18
  20.4 5.9 %collective-permute-done = bf16[1,1,64,16,128]{4,2,3,1,0:T(8,128)(2,1)S(1)} collective-permute-done((bf16[1,1,64,16,128]{4,2,3,1,0:T(8,128)(2,1)S(1)}, bf16[1,1,64,16,128]{4,2,3,1,0:T(8,128)(2,1)S(1)}, u32[]{:S(2)}, u32[]{:S(2)}) %collective-permute-start) | collective-permute-done | bytes 262176 | tf_op jit(solution)/shard_map/ppermute | solution.py:17
  26.3 0.4 select_maximum_fusion
  26.7 0.3 fusion.175
  27.0 2.5 %fusion.174 = (bf16[1,1,64,16,128]{4,2,3,1,0:T(8,128)(2,1)}, bf16[1,1,64,16,128]{4,2,3,1,0:T(8,128)(2,1)}, bf16[1,1,64,16,128]{4,2,3,1,0:T(8,128)(2,1)}, bf16[1,...) fusion(bf16[1,3,66,18,128]{4,2,3,1,0:T(8,128)(2,1)S(1)} %select, ...), kind=kLoop, calls=%fused_computation.235 | loop fusion | bytes 9961472 | tf_op jit(solution)/shard_map/slice | solution.py:47
  29.5 0.9 copy.161
  30.6 0.9 copy.160
  31.5 0.9 copy.159
  32.5 1.0 fusion.86
  33.5 1.0 fusion.92
  34.5 0.3 fusion.32
  34.8 0.3 fusion.31
  35.3 0.3 fusion.29
  35.9 0.3 fusion.27
  37.2 0.3 fusion.22
  37.5 0.3 fusion.21
  38.3 0.3 fusion.18
  40.0 0.3 fusion.12
  40.8 0.3 fusion.9
  42.1 2.1 copy.212
  44.2 0.9 copy-done.21
  54.5 0.3 copy-done.3
  56.0 0.9 fusion.5
  56.9 120.6 %all-reduce.4.cloned.1.call-done = f32[442368]{0:T(1024)} async-done(((f32[442368]{0:T(1024)}), f32[442368]{0:T(1024)}) %all-reduce.4.cloned.1.call-update) | async-done | bytes 1769488
  177.5 1.6 fusion.172
  179.1 45.6 %all-gather = bf16[32,1,13824]{2,1,0:T(2,128)(2,1)S(1)} all-gather(bf16[1,1,13824]{2,1,0:T(2,128)(2,1)S(1)} %reshape.280), channel_id=1, replica_groups=mesh['depth'=16,'samp'=2] {'depth','samp'}, dimensions={0}, use_global_device_ids=true | all-gather | bytes 912384 | tf_op jit(solution)/shard_map/all_gather | solution.py:69
  224.7 5.3 %reduce = bf16[32,13824]{1,0:T(8,128)(2,1)S(1)} reduce(bf16[32,1,13824]{2,1,0:T(2,128)(2,1)S(1)} %all-gather, bf16[]{:T(256)} %constant.33), dimensions={1}, to_apply=%all-gather.reduce_sub_computation | reduce | bytes 1769474 | tf_op jit(solution)/shard_map/all_gather | solution.py:69
  230.0 2.3 reshape.279
  (127 shorter events, 15.4 us)
Async XLA Ops:
  7.2 27.3 %copy-start = (bf16[1,1,64,16,128]{4,3,2,1,0:T(8,128)(2,1)S(1)}, bf16[1,1,64,16,128]{4,3,2,1,0:T(8,128)(2,1)}, u32[]{:S(2)}) copy-start(bf16[1,1,64,16,128]{4,3,2,1,0:T(8,128)(2,1)} %param.7) | copy-start | bytes 786436
  7.2 170.3 %all-reduce.4.cloned.1.call-start = ((), (), s32[]{:S(2)}) async-start(), calls=%async_computation | async-start | bytes 3538944
  8.4 12.0 %collective-permute-start.1 = (bf16[1,1,64,16,128]{4,2,3,1,0:T(8,128)(2,1)S(1)}, bf16[1,1,64,16,128]{4,2,3,1,0:T(8,128)(2,1)S(1)}, u32[]{:S(2)}, u32[]{:S(2)}) collective-permute-start(bf16[1,1,64,16,128]{4,2,3,1,0:T(8,128)(2,1)S(1)} %multiply_convert_fusion), channel_id=1, source_target_pairs={{2,0},{4,2},{6,4},{8,6},{10,8},{12,10},{14,12},{16,14},{18,16},{20... | collective-permute-start | bytes 786440 | tf_op jit(solution)/shard_map/ppermute | solution.py:18
  9.7 16.6 %collective-permute-start = (bf16[1,1,64,16,128]{4,2,3,1,0:T(8,128)(2,1)S(1)}, bf16[1,1,64,16,128]{4,2,3,1,0:T(8,128)(2,1)S(1)}, u32[]{:S(2)}, u32[]{:S(2)}) collective-permute-start(bf16[1,1,64,16,128]{4,2,3,1,0:T(8,128)(2,1)S(1)} %multiply_convert_fusion), channel_id=1, source_target_pairs={{0,2},{2,4},{4,6},{6,8},{8,10},{10,12},{12,14},{14,16},{16,18},{18... | collective-permute-start | bytes 786440 | tf_op jit(solution)/shard_map/ppermute | solution.py:17
  20.4 15.2 %copy-start.4 = (bf16[1,1,64,16,128]{4,2,3,1,0:T(8,128)(2,1)}, bf16[1,1,64,16,128]{4,2,3,1,0:T(8,128)(2,1)S(1)}, u32[]{:S(2)}) copy-start(bf16[1,1,64,16,128]{4,2,3,1,0:T(8,128)(2,1)S(1)} %collective-permute-done.1) | copy-start | bytes 786436
  44.2 1.3 copy-start.26
  44.2 1.5 copy-start.20
  44.2 1.7 copy-start.19
  44.2 1.9 copy-start.18
  44.2 2.0 copy-start.17
  44.2 2.2 copy-start.16
  45.3 1.4 copy-start.15
  45.7 1.2 copy-start.14
  45.7 1.4 copy-start.13
  45.9 1.4 copy-start.12
  46.1 1.4 copy-start.11
  46.3 1.4 copy-start.10
  46.5 1.4 copy-start.9
  46.7 1.4 copy-start.8
  46.9 1.4 copy-start.7
  47.1 1.4 copy-start.6
  47.3 1.4 copy-start.25
  47.9 1.0 copy-start.24
  48.3 1.0 copy-start.23
  48.7 1.0 copy-start.5
  51.0 1.0 copy-start.22
  53.9 1.0 copy-start.3
  54.1 1.0 copy-start.2
  54.1 1.1 copy-start.1
  55.4 122.0 %copy-start.27 = (f32[13824]{0:T(1024)S(1)}, f32[13824]{0:T(1024)}, u32[]{:S(2)}) copy-start(f32[13824]{0:T(1024)} %param.11) | copy-start | bytes 165892
  55.5 122.0 %copy-start.28 = (f32[13824]{0:T(1024)S(1)}, f32[13824]{0:T(1024)}, u32[]{:S(2)}) copy-start(f32[13824]{0:T(1024)} %param.13) | copy-start | bytes 165892
  55.5 122.0 %copy-start.29 = (f32[13824]{0:T(1024)S(1)}, f32[13824]{0:T(1024)}, u32[]{:S(2)}) copy-start(f32[13824]{0:T(1024)} %param.12) | copy-start | bytes 165892
  (1 other events, 0.9 us)
Sparse Core Ops, SparseCore 0:
  44.3 133.0 all-reduce.3
where the time goes:
time: 240 us; the launch traced here: 239 us
  waiting for transfers between devices  131 us (55%)
  blocking collectives  45.6 us (19%)
  local copies, waits for them, and re-layouts  16.8 us (7%)
  matrix products  15.6 us (6%)
  between operations  14.9 us (6%)
  other arithmetic  8.65 us (4%)
  starting transfers between devices  6.84 us (3%)
    unnamed x2, waiting for transfers between devices  121 us
    all_gather x1, blocking collectives, local(): whole = lax.all_gather(share, ('depth', 'samp'), axis=0, tiled=True)  45.6 us
    slice x26, local copies, waits for them, and re-layouts, local(): padded_cot[:, 2 - depth_tap:2 - depth_tap + planes, 2 - row_tap:2 - row_t...  9.12 us
    dot_general x27, matrix products, local(): jnp.dot(cot_rows, weights[depth_tap, row_tap, col_tap].T, preferred_eleme...  8.36 us
    dot_general x27, matrix products, contract_rows(): lax.dot_general(left, right, (((0,), (0,)), ((), ())), preferred_element_...  7.22 us
    ppermute x1, waiting for transfers between devices, padded(): before = lax.ppermute(last, axis, up)  5.87 us
    ppermute x1, starting transfers between devices, padded(): before = lax.ppermute(last, axis, up)  5.52 us
    all_gather x1, other arithmetic, local(): whole = lax.all_gather(share, ('depth', 'samp'), axis=0, tiled=True)  5.32 us
  transfers between devices with their start and end apart: 3, of which 3 were waited for; matrix products, arithmetic and copies ran while one was open for 5% of the time, Pallas kernels for 0%

commit v1 on v0

v1 whole, which is shorter than its diff:
```python
import functools
import jax
import jax.numpy as jnp
from jax import lax
from jax.experimental import pallas as pl
from jax.experimental.pallas import tpu as pltpu
from jax.sharding import PartitionSpec as P

first_fix = 1.0
second_fix = 0.63230457524
AXES = ("depth", "samp")
VMEM = pl.BlockSpec(memory_space=pltpu.VMEM)
SMEM = pl.BlockSpec(memory_space=pltpu.SMEM)


def call(body, outs, n_in, flops=0, moved=0, scratch=(), limit=24 << 20):
    return pl.pallas_call(
        body,
        out_shape=outs,
        in_specs=[SMEM] + [VMEM] * n_in,
        out_specs=jax.tree.map(lambda _: VMEM, outs),
        scratch_shapes=list(scratch),
        cost_estimate=pl.CostEstimate(flops=flops, bytes_accessed=moved, transcendentals=0),
        compiler_params=pltpu.CompilerParams(vmem_limit_bytes=limit),
    )


def fill_shifted(shifted, slot, plane, width):
    rows, chans = plane.shape
    wide = plane.astype(jnp.float32)
    column = lax.broadcasted_iota(jnp.int32, (rows, chans), 0) % width
    nxt = jnp.where(column == width - 1, 0.0, pltpu.roll(wide, rows - 1, 0))
    prv = jnp.where(column == 0, 0.0, pltpu.roll(wide, 1, 0))
    edge = jnp.zeros((width, 3 * chans), plane.dtype)
    shifted[slot, 0:width, :] = edge
    shifted[slot, width + rows : 2 * width + rows, :] = edge
    body = slice(width, width + rows)
    shifted[slot, body, 0:chans] = nxt.astype(plane.dtype)
    shifted[slot, body, chans : 2 * chans] = plane
    shifted[slot, body, 2 * chans :] = prv.astype(plane.dtype)


def filter_body(width, pieces, step, me, act, cot, before, after, keep, send, shifted, grads):
    rows, chans = cot.shape
    left = act[...]
    for slot, plane in ((1, cot), (0, after), (2, before)):
        fill_shifted(shifted, slot, plane[...], width)
        for b in range(3):
            part = shifted[slot, (2 - b) * width : (2 - b) * width + rows, :]
            out = lax.dot_general(
                left, part, (((0,), (0,)), ((), ())), preferred_element_type=jnp.float32
            )
            for c in range(3):
                tap = (slot * 3 + b) * 3 + c
                grads[tap * chans : (tap + 1) * chans, :] = out[:, c * chans : (c + 1) * chans]
    chip = grads.shape[0] // pieces
    wide = keep.shape[1]
    mine = me[0] * step
    other = (1 - me[0]) * step
    for k in range(pieces):
        keep[k] = grads[pl.ds(pl.multiple_of(k * chip + mine, 8), wide), :]
        send[k] = grads[pl.ds(pl.multiple_of(k * chip + other, 8), wide), :]


def all_filter_body(width, me, act, cot, before, after, grads, shifted):
    rows, chans = cot.shape
    left = act[...]
    for slot, plane in ((1, cot), (0, after), (2, before)):
        fill_shifted(shifted, slot, plane[...], width)
        for b in range(3):
            part = shifted[slot, (2 - b) * width : (2 - b) * width + rows, :]
            out = lax.dot_general(
                left, part, (((0,), (0,)), ((), ())), preferred_element_type=jnp.float32
            )
            for c in range(3):
                tap = (slot * 3 + b) * 3 + c
                grads[tap * chans : (tap + 1) * chans, :] = out[:, c * chans : (c + 1) * chans]


def input_body(width, me, cot, before, after, weights, out, shifted):
    rows, chans = cot.shape
    total = jnp.zeros((rows, chans), jnp.float32)
    for slot, plane in ((1, cot), (0, after), (2, before)):
        fill_shifted(shifted, slot, plane[...], width)
        for b in range(3):
            part = shifted[slot, (2 - b) * width : (2 - b) * width + rows, :]
            taps = [weights[(slot * 3 + b) * 3 + c] for c in range(3)]
            total = total + lax.dot_general(
                part,
                jnp.concatenate(taps, axis=1),
                (((1,), (1,)), ((), ())),
                preferred_element_type=jnp.float32,
            )
    out[...] = total.astype(out.dtype)


def merge_body(n, me, *refs):
    terms, outs = refs[: len(refs) - n], refs[len(refs) - n :]
    place = me[0]
    for m in range(n):
        at = place ^ m
        for z in range(outs[m].shape[0]):
            total = terms[0][z * n + at]
            for term in terms[1:]:
                total = total + term[z * n + at]
            outs[m][z] = total


def adam_body(step, count, me, *refs):
    terms, (master, moment, second), outs = refs[:-8], refs[-8:-5], refs[-5:]
    total = terms[0][0]
    for term in terms[1:]:
        total = total + term[0]
    size = master.shape[0]
    skip = total.shape[0] - size
    raw = jnp.where(me[0] == 0, total[0:size], total[skip : skip + size])
    grad = raw * jnp.float32(1.0 / count**0.5)
    new_moment = 0.9 * moment[...] + 0.1 * grad
    new_second = 0.999 * second[...] + 0.001 * grad * grad
    new_master = master[...] - 0.01 * (new_moment / first_fix) / (
        jnp.sqrt(new_second / second_fix) + 1e-08
    )
    outs[0][...] = grad
    outs[1][...] = new_moment
    outs[2][...] = new_second
    outs[3][...] = new_master
    outs[4][0, 0:size, :] = new_master.astype(jnp.bfloat16)
    outs[4][0, size:, :] = jnp.zeros((outs[4].shape[1] - size, master.shape[1]), jnp.bfloat16)


def gather_body(me, *refs):
    for k, ref in enumerate(refs[:-1]):
        refs[-1][k] = ref[0]


def place_body(fast, slow, size, me, *refs):
    own, peer, out, held, wide = refs[:fast], refs[fast : 2 * fast], refs[-3], refs[-2], refs[-1]
    for m in range(fast):
        held[0, m] = own[m][...]
        held[1, m] = peer[m][...]
    for z in range(slow):
        for k in range(fast):
            for c in range(2):
                block = held[c ^ me[2], k ^ me[1], z ^ me[0]]
                at = ((z * fast + k) * 2 + c) * size
                wide[at : at + size, :] = block[0:size].astype(jnp.float32)
    out[...] = wide[...].astype(out.dtype)


def swap(array, axis, mask):
    return lax.ppermute(array, axis, [(i, i ^ mask) for i in range(lax.axis_size(axis))])


def staged(groups, act, cot, before, after, weights, states, width, count):
    fast, slow = groups
    chans = act.shape[1]
    rows = 27 * chans
    size = rows // (2 * fast * slow)
    chip = 2 * size
    wide = -(-size // 16) * 16
    step = chip - wide
    core, depth = lax.axis_index("samp"), lax.axis_index("depth")
    one = lambda value: jnp.reshape(value, (1,)).astype(jnp.int32)
    fast_at, slow_at = depth % fast, depth // fast
    f32 = lambda *shape: jax.ShapeDtypeStruct(shape, jnp.float32)
    b16 = lambda *shape: jax.ShapeDtypeStruct(shape, jnp.bfloat16)
    pieces = fast * slow
    shift_rows = cot.shape[0] + 2 * width
    half = f32(pieces, wide, chans)
    keep, send = call(
        functools.partial(filter_body, width, pieces, step),
        (half, half),
        4,
        flops=2 * rows * chans * cot.shape[0],
        scratch=[
            pltpu.VMEM((3, shift_rows, 3 * chans), jnp.bfloat16),
            pltpu.VMEM((rows, chans), jnp.float32),
        ],
    )(one(core), act, cot, before, after)
    come = swap(send, "samp", 1)
    parts = call(functools.partial(merge_body, fast), (f32(slow, wide, chans),) * fast, 2)(
        one(fast_at), keep, come
    )
    got = [parts[0]] + [swap(parts[m], "depth", m) for m in range(1, fast)]
    parts = call(functools.partial(merge_body, slow), (f32(1, wide, chans),) * slow, fast)(
        one(slow_at), *got
    )
    got = [parts[0]] + [swap(parts[m], "depth", m * fast) for m in range(1, slow)]
    grad_input = call(
        functools.partial(input_body, width),
        b16(*cot.shape),
        4,
        flops=2 * rows * chans * cot.shape[0],
        moved=4 << 20,
        scratch=[pltpu.VMEM((3, shift_rows, 3 * chans), jnp.bfloat16)],
    )(one(core), cot, before, after, weights)
    flat = f32(size, chans)
    states = [s.reshape(size, chans) for s in states]
    *fresh, share = call(
        functools.partial(adam_body, step, count), (flat,) * 4 + (b16(1, wide, chans),), slow + 3
    )(one(core), *got, *states)
    got = [share] + [swap(share, "depth", m * fast) for m in range(1, slow)]
    line = call(gather_body, b16(slow, wide, chans), slow)(one(core), *got)
    own = [line] + [swap(line, "depth", m) for m in range(1, fast)]
    peer = [swap(block, "samp", 1) for block in own]
    new_weights = call(
        functools.partial(place_body, fast, slow, size),
        b16(rows, chans),
        2 * fast,
        scratch=[
            pltpu.VMEM((2, fast, slow, wide, chans), jnp.bfloat16),
            pltpu.VMEM((rows, chans), jnp.float32),
        ],
    )(jnp.stack([slow_at, fast_at, core]).astype(jnp.int32), *own, *peer)
    return grad_input, [x.reshape(-1) for x in fresh], new_weights


def plain(act, cot, before, after, weights, states, width, count):
    chans = act.shape[1]
    rows = 27 * chans
    shift = pltpu.VMEM((3, cot.shape[0] + 2 * width, 3 * chans), jnp.bfloat16)
    core = jnp.reshape(lax.axis_index("samp"), (1,)).astype(jnp.int32)
    grads = call(
        functools.partial(all_filter_body, width),
        jax.ShapeDtypeStruct((rows, chans), jnp.float32),
        4,
        scratch=[shift],
    )(core, act, cot, before, after)
    grad_input = call(
        functools.partial(input_body, width),
        jax.ShapeDtypeStruct(cot.shape, jnp.bfloat16),
        4,
        scratch=[shift],
    )(core, cot, before, after, weights)
    total = lax.psum_scatter(grads.reshape(-1), AXES, scatter_dimension=0, tiled=True)
    master, moment, second = states
    grad = total * jnp.float32(1.0 / count**0.5)
    new_moment = 0.9 * moment + 0.1 * grad
    new_second = 0.999 * second + 0.001 * grad * grad
    new_master = master - 0.01 * (new_moment / first_fix) / (
        jnp.sqrt(new_second / second_fix) + 1e-08
    )
    whole = lax.all_gather(new_master.astype(jnp.bfloat16), AXES, axis=0, tiled=True)
    return grad_input, [grad, new_moment, new_second, new_master], whole


def local(groups, activations, preact, out_grad, weights, master, moment, second):
    samples, planes, height, width, chans = activations.shape
    count = samples * lax.axis_size("samp") * planes * lax.axis_size("depth") * height * width
    peers = lax.axis_size("depth")
    slope = jnp.where(preact > 0, jnp.float32(1.0), jnp.float32(0.01))
    cot = (out_grad.astype(jnp.float32) * slope).astype(jnp.bfloat16).reshape(-1, chans)
    act = activations.reshape(-1, chans)
    up = [(i, i + 1) for i in range(peers - 1)]
    before = lax.ppermute(cot, "depth", up)
    after = lax.ppermute(cot, "depth", [(j, i) for i, j in up])
    taps = weights.reshape(27, chans, chans)
    states = (master, moment, second)
    if groups:
        result = staged(groups, act, cot, before, after, taps, states, width, count)
    else:
        result = plain(act, cot, before, after, taps, states, width, count)
    grad_input, fresh, whole = result
    return (grad_input.reshape(activations.shape), *fresh, whole.reshape(weights.shape))


def stages(mesh):
    depth, samp = mesh.shape["depth"], mesh.shape["samp"]
    slow = 1
    while slow * slow < depth:
        slow *= 2
    if samp != 2 or slow * slow != depth:
        return None
    return depth // slow, slow


def solution(mesh):
    split = P("samp", "depth", None, None, None)
    shard = P(AXES)
    return jax.shard_map(
        functools.partial(local, stages(mesh)),
        mesh=mesh,
        in_specs=(split, split, split, P(), shard, shard, shard),
        out_specs=(split, shard, shard, shard, shard, P()),
        check_vma=False,
    )
```

time: 240 us -> 69.6 us (0.29)
  waiting for transfers between devices: 131 us -> 37.2 us
  blocking collectives: 45.6 us -> 0 us
  local copies, waits for them, and re-layouts: 16.8 us -> 0.03 us
  matrix products: 15.6 us -> 0 us
  starting transfers between devices: 6.84 us -> 22.1 us
  between operations: 14.9 us -> 0.76 us
  Pallas kernels: 0 us -> 8.08 us
  other arithmetic: 8.65 us -> 1.25 us
    unnamed x2 -> x0, waiting for transfers between devices: 121 us -> none
    all_gather x1 -> x0, blocking collectives: 45.6 us -> none  [local(): whole = lax.all_gather(share, ('depth', 'samp'), axis=0, tiled=True)]
    ppermute x2 -> x19, waiting for transfers between devices: 10.2 us -> 37.2 us  [the longest x17 25.4 us: swap(): lax.ppermute(array, axis, [(i, i ^ mask) for i in range(lax.axis_size(axi...]
    dot_general x54 -> x0, matrix products: 15.6 us -> none  [the longest x27 8.36 us: local(): jnp.dot(cot_rows, weights[depth_tap, row_tap, col_tap].T, preferred_eleme...]
    ppermute x2 -> x19, starting transfers between devices: 6.81 us -> 22.1 us  [the longest x17 16 us: swap(): lax.ppermute(array, axis, [(i, i ^ mask) for i in range(lax.axis_size(axi...]
    slice x26 -> x0, local copies, waits for them, and re-layouts: 9.12 us -> none  [local(): padded_cot[:, 2 - depth_tap:2 - depth_tap + planes, 2 - row_tap:2 - row_t...]
    pallas_call x0 -> x7, Pallas kernels: none -> 8.08 us  [the longest x1 2.85 us: staged(): call(functools.partial(input_body, width), b16(*cot.shape), 4, flops=2 *...]
    all_gather x1 -> x0, other arithmetic: 5.32 us -> none  [local(): whole = lax.all_gather(share, ('depth', 'samp'), axis=0, tiled=True)]
  transfers between devices with their start and end apart: 3 -> 19, of which waited for: 3 -> 13; matrix products, arithmetic and copies ran while one was open for 5% -> 0% of each run, Pallas kernels for 0% -> 4%
where the time goes in v1:
time: 69.6 us; the launch traced here: 69.4 us
  waiting for transfers between devices  37.2 us (53%)
  starting transfers between devices  22.1 us (32%)
  Pallas kernels  8.08 us (12%)
  other arithmetic  1.25 us (2%)
  between operations  0.76 us (1%)
    ppermute x17, waiting for transfers between devices, swap(): lax.ppermute(array, axis, [(i, i ^ mask) for i in range(lax.axis_size(axi...  25.4 us
    ppermute x17, starting transfers between devices, swap(): lax.ppermute(array, axis, [(i, i ^ mask) for i in range(lax.axis_size(axi...  16 us
    ppermute x1, waiting for transfers between devices, local(): before = lax.ppermute(cot, 'depth', up)  9.88 us
    ppermute x1, starting transfers between devices, local(): before = lax.ppermute(cot, 'depth', up)  4.89 us
    pallas_call x1, Pallas kernels, staged(): call(functools.partial(input_body, width), b16(*cot.shape), 4, flops=2 *...  2.85 us
    ppermute x1, waiting for transfers between devices, local(): after = lax.ppermute(cot, 'depth', [(j, i) for i, j in up])  1.91 us
    pallas_call x1, Pallas kernels, staged(): call(functools.partial(filter_body, width, pieces, step), (half, half), 4...  1.84 us
    pallas_call x1, Pallas kernels, staged(): call(functools.partial(place_body, fast, slow, size), b16(rows, chans), 2...  1.71 us
  transfers between devices with their start and end apart: 19, of which 13 were waited for; matrix products, arithmetic and copies ran while one was open for 0% of the time, Pallas kernels for 4%

profile of v1, /device:TPU:0, one launch (start us, length us, event | category | flops | bytes accessed | tf_op | source)
XLA Modules:
  0.0 69.4 jit_solution(12518075473684776031)
XLA Ops:
  0.6 1.2 %multiply_convert_fusion = bf16[1,1,64,16,128]{4,3,2,1,0:T(8,128)(2,1)S(1)} fusion(bf16[1,1,64,16,128]{4,3,2,1,0:T(8,128)(2,1)} %param.9, bf16[1,1,64,16,128]{4,3,2,1,0:T(8,128)(2,1)} %param.8), kind=kLoop, calls=%fused_computation | loop fusion | flops 655360 | bytes 786432 | tf_op jit(solution)/shard_map/convert_element_type | solution.py:252
  1.8 4.9 %collective-permute-start = (bf16[1024,128]{1,0:T(8,128)(2,1)S(1)}, bf16[1024,128]{1,0:T(8,128)(2,1)S(1)}, u32[]{:S(2)}, u32[]{:S(2)}) collective-permute-start(bf16[1024,128]{1,0:T(8,128)(2,1)S(1)} %bitcast.15), channel_id=1, source_target_pairs={{0,2},{2,4},{4,6},{6,8},{8,10},{10,12},{12,14},{14,16},{16,18},{18... | collective-permute-start | bytes 786440 | tf_op jit(solution)/shard_map/ppermute | solution.py:255
  6.7 1.3 %collective-permute-start.1 = (bf16[1024,128]{1,0:T(8,128)(2,1)S(1)}, bf16[1024,128]{1,0:T(8,128)(2,1)S(1)}, u32[]{:S(2)}, u32[]{:S(2)}) collective-permute-start(bf16[1024,128]{1,0:T(8,128)(2,1)S(1)} %bitcast.16), channel_id=1, source_target_pairs={{2,0},{4,2},{6,4},{8,6},{10,8},{12,10},{14,12},{16,14},{18,16},{20... | collective-permute-start | bytes 786440 | tf_op jit(solution)/shard_map/ppermute | solution.py:256
  8.0 9.9 %collective-permute-done.before = bf16[1024,128]{1,0:T(8,128)(2,1)S(1)} collective-permute-done((bf16[1024,128]{1,0:T(8,128)(2,1)S(1)}, bf16[1024,128]{1,0:T(8,128)(2,1)S(1)}, u32[]{:S(2)}, u32[]{:S(2)}) %collective-permute-start) | collective-permute-done | bytes 262176 | tf_op jit(solution)/shard_map/ppermute | solution.py:255
  17.9 1.9 %collective-permute-done.1.after = bf16[1024,128]{1,0:T(8,128)(2,1)S(1)} collective-permute-done((bf16[1024,128]{1,0:T(8,128)(2,1)S(1)}, bf16[1024,128]{1,0:T(8,128)(2,1)S(1)}, u32[]{:S(2)}, u32[]{:S(2)}) %collective-permute-start.1) | collective-permute-done | bytes 262176 | tf_op jit(solution)/shard_map/ppermute | solution.py:256
  19.8 1.8 %shard_map.119 = (f32[16,112,128]{2,1,0:T(8,128)S(1)}, f32[16,112,128]{2,1,0:T(8,128)S(1)}) custom-call(s32[1]{0:T(128)} %bitcast.me, bf16[1024,128]{1,0:T(8,128)(2,1)S(1)} %bitcast.23, bf16[1024,128]{1,0:T(8,128)(2,1)S(1)} %bitcast.17, bf16[1024,128]{1,0:T(8,128)(2,1)S(1)} %collective-permute-done.before, bf16[1024,128]{1,0:T(8,128)(2,1)S(1)} %collective-permute-done.1.after), custom_call_target="tpu_custom_call" | custom-call | flops 905969664 | tf_op jit(solution)/shard_map/pallas_call | solution.py:170
  21.8 2.4 %collective-permute-done.2.refs_1_ = f32[16,112,128]{2,1,0:T(8,128)S(1)} collective-permute-done((f32[16,112,128]{2,1,0:T(8,128)S(1)}, f32[16,112,128]{2,1,0:T(8,128)S(1)}, u32[]{:S(2)}, u32[]{:S(2)}) %collective-permute-start.2) | collective-permute-done | bytes 917536 | tf_op jit(solution)/shard_map/ppermute | solution.py:151
  24.2 0.9 %shard_map.120 = (f32[4,112,128]{2,1,0:T(8,128)S(1)}, f32[4,112,128]{2,1,0:T(8,128)}, f32[4,112,128]{2,1,0:T(8,128)}, f32[4,112,128]{2,1,0:T(8,128)}) custom-call(s32[1]{0:T(128)} %bitcast.5.me, f32[16,112,128]{2,1,0:T(8,128)S(1)} %get-tuple-element.21.refs_0_, f32[16,112,128]{2,1,0:T(8,128)S(1)} %collective-permute-done.2.refs_1_), custom_call_target="tpu_custom_call" | custom-call | tf_op jit(solution)/shard_map/pallas_call | solution.py:181
  25.1 1.5 %collective-permute-start.3 = (f32[4,112,128]{2,1,0:T(8,128)}, f32[4,112,128]{2,1,0:T(8,128)S(1)}, u32[]{:S(2)}, u32[]{:S(2)}) collective-permute-start(f32[4,112,128]{2,1,0:T(8,128)} %get-tuple-element.24), channel_id=1, source_target_pairs={{0,2},{2,0},{4,6},{6,4},{8,10},{10,8},{12,14},{14,12},{16,18},{18,... | collective-permute-start | bytes 688136 | tf_op jit(solution)/shard_map/ppermute | solution.py:151
  26.6 2.0 %collective-permute-start.5 = (f32[4,112,128]{2,1,0:T(8,128)}, f32[4,112,128]{2,1,0:T(8,128)S(1)}, u32[]{:S(2)}, u32[]{:S(2)}) collective-permute-start(f32[4,112,128]{2,1,0:T(8,128)} %get-tuple-element.26), channel_id=1, source_target_pairs={{0,6},{2,4},{4,2},{6,0},{8,14},{10,12},{12,10},{14,8},{16,22},{18,... | collective-permute-start | bytes 688136 | tf_op jit(solution)/shard_map/ppermute | solution.py:151
  28.6 5.2 %collective-permute-done.3.refs_1_ = f32[4,112,128]{2,1,0:T(8,128)S(1)} collective-permute-done((f32[4,112,128]{2,1,0:T(8,128)}, f32[4,112,128]{2,1,0:T(8,128)S(1)}, u32[]{:S(2)}, u32[]{:S(2)}) %collective-permute-start.3) | collective-permute-done | bytes 229408 | tf_op jit(solution)/shard_map/ppermute | solution.py:151
  33.8 5.3 %collective-permute-done.4.refs_2_ = f32[4,112,128]{2,1,0:T(8,128)S(1)} collective-permute-done((f32[4,112,128]{2,1,0:T(8,128)}, f32[4,112,128]{2,1,0:T(8,128)S(1)}, u32[]{:S(2)}, u32[]{:S(2)}) %collective-permute-start.4) | collective-permute-done | bytes 229408 | tf_op jit(solution)/shard_map/ppermute | solution.py:151
  39.2 1.6 %collective-permute-start.6 = (f32[1,112,128]{2,1,0:T(8,128)S(1)}, f32[1,112,128]{2,1,0:T(8,128)S(1)}, u32[]{:S(2)}, u32[]{:S(2)}) collective-permute-start(f32[1,112,128]{2,1,0:T(8,128)S(1)} %get-tuple-element.28), channel_id=1, source_target_pairs={{0,8},{2,10},{4,12},{6,14},{8,0},{10,2},{12,4},{14,6},{16,24},{18,... | collective-permute-start | bytes 172040 | tf_op jit(solution)/shard_map/ppermute | solution.py:151
  40.8 2.6 %collective-permute-start.7 = (f32[1,112,128]{2,1,0:T(8,128)S(1)}, f32[1,112,128]{2,1,0:T(8,128)S(1)}, u32[]{:S(2)}, u32[]{:S(2)}) collective-permute-start(f32[1,112,128]{2,1,0:T(8,128)S(1)} %get-tuple-element.29), channel_id=1, source_target_pairs={{0,16},{2,18},{4,20},{6,22},{8,24},{10,26},{12,28},{14,30},{16,0},... | collective-permute-start | bytes 172040 | tf_op jit(solution)/shard_map/ppermute | solution.py:151
  43.4 0.2 collective-permute-start.8
  43.6 0.3 collective-permute-done.6.refs_1_
  44.0 3.2 %collective-permute-done.7.refs_2_ = f32[1,112,128]{2,1,0:T(8,128)S(1)} collective-permute-done((f32[1,112,128]{2,1,0:T(8,128)S(1)}, f32[1,112,128]{2,1,0:T(8,128)S(1)}, u32[]{:S(2)}, u32[]{:S(2)}) %collective-permute-start.7) | collective-permute-done | bytes 57376 | tf_op jit(solution)/shard_map/ppermute | solution.py:151
  47.1 2.3 %collective-permute-done.8.refs_3_ = f32[1,112,128]{2,1,0:T(8,128)S(1)} collective-permute-done((f32[1,112,128]{2,1,0:T(8,128)S(1)}, f32[1,112,128]{2,1,0:T(8,128)S(1)}, u32[]{:S(2)}, u32[]{:S(2)}) %collective-permute-start.8) | collective-permute-done | bytes 57376 | tf_op jit(solution)/shard_map/ppermute | solution.py:151
  49.4 0.7 %shard_map.122 = (f32[108,128]{1,0:T(8,128)}, f32[108,128]{1,0:T(8,128)}, f32[108,128]{1,0:T(8,128)}, f32[108,128]{1,0:T(8,128)}, bf16[1,112,128]{2,1,0:T(8,128)(2,1)S(1)}) custom-call(s32[1]{0:T(128)} %bitcast.me, f32[1,112,128]{2,1,0:T(8,128)S(1)} %get-tuple-element.27.refs_0_, f32[1,112,128]{2,1,0:T(8,128)S(1)} %collective-permute-done.6.refs_1_, ...), custom_call_target="tpu_custom_call" | custom-call | tf_op jit(solution)/shard_map/pallas_call | solution.py:199
  50.1 1.3 %collective-permute-start.10 = (bf16[1,112,128]{2,1,0:T(8,128)(2,1)S(1)}, bf16[1,112,128]{2,1,0:T(8,128)(2,1)S(1)}, u32[]{:S(2)}, u32[]{:S(2)}) collective-permute-start(bf16[1,112,128]{2,1,0:T(8,128)(2,1)S(1)} %get-tuple-element.35.refs_0_), channel_id=1, source_target_pairs={{0,16},{2,18},{4,20},{6,22},{8,24},{10,26},{12,28},{14,30},{16,0},... | collective-permute-start | bytes 86024 | tf_op jit(solution)/shard_map/ppermute | solution.py:151
  51.4 3.1 %collective-permute-start.11 = (bf16[1,112,128]{2,1,0:T(8,128)(2,1)S(1)}, bf16[1,112,128]{2,1,0:T(8,128)(2,1)S(1)}, u32[]{:S(2)}, u32[]{:S(2)}) collective-permute-start(bf16[1,112,128]{2,1,0:T(8,128)(2,1)S(1)} %get-tuple-element.35.refs_0_), channel_id=1, source_target_pairs={{0,24},{2,26},{4,28},{6,30},{8,16},{10,18},{12,20},{14,22},{16,8},... | collective-permute-start | bytes 86024 | tf_op jit(solution)/shard_map/ppermute | solution.py:151
  54.5 0.4 collective-permute-done.10.refs_2_
  54.9 2.2 %collective-permute-done.11.refs_3_ = bf16[1,112,128]{2,1,0:T(8,128)(2,1)S(1)} collective-permute-done((bf16[1,112,128]{2,1,0:T(8,128)(2,1)S(1)}, bf16[1,112,128]{2,1,0:T(8,128)(2,1)S(1)}, u32[]{:S(2)}, u32[]{:S(2)}) %collective-permute-start.11) | collective-permute-done | bytes 28704 | tf_op jit(solution)/shard_map/ppermute | solution.py:151
  57.1 0.6 collective-permute-start.12
  57.7 1.4 %collective-permute-start.13 = (bf16[4,112,128]{2,1,0:T(8,128)(2,1)S(1)}, bf16[4,112,128]{2,1,0:T(8,128)(2,1)S(1)}, u32[]{:S(2)}, u32[]{:S(2)}) collective-permute-start(bf16[4,112,128]{2,1,0:T(8,128)(2,1)S(1)} %shard_map.123.refs_0_), channel_id=1, source_target_pairs={{0,4},{2,6},{4,0},{6,2},{8,12},{10,14},{12,8},{14,10},{16,20},{18,... | collective-permute-start | bytes 344072 | tf_op jit(solution)/shard_map/ppermute | solution.py:151
  59.1 1.5 %collective-permute-start.14 = (bf16[4,112,128]{2,1,0:T(8,128)(2,1)S(1)}, bf16[4,112,128]{2,1,0:T(8,128)(2,1)S(1)}, u32[]{:S(2)}, u32[]{:S(2)}) collective-permute-start(bf16[4,112,128]{2,1,0:T(8,128)(2,1)S(1)} %shard_map.123.refs_0_), channel_id=1, source_target_pairs={{0,6},{2,4},{4,2},{6,0},{8,14},{10,12},{12,10},{14,8},{16,22},{18,... | collective-permute-start | bytes 344072 | tf_op jit(solution)/shard_map/ppermute | solution.py:151
  60.6 1.3 %collective-permute-done.12.refs_1_ = bf16[4,112,128]{2,1,0:T(8,128)(2,1)S(1)} collective-permute-done((bf16[4,112,128]{2,1,0:T(8,128)(2,1)S(1)}, bf16[4,112,128]{2,1,0:T(8,128)(2,1)S(1)}, u32[]{:S(2)}, u32[]{:S(2)}) %collective-permute-start.12) | collective-permute-done | bytes 114720 | tf_op jit(solution)/shard_map/ppermute | solution.py:151
  61.9 0.5 collective-permute-done.13.refs_2_
  62.5 2.3 %collective-permute-done.14.refs_3_ = bf16[4,112,128]{2,1,0:T(8,128)(2,1)S(1)} collective-permute-done((bf16[4,112,128]{2,1,0:T(8,128)(2,1)S(1)}, bf16[4,112,128]{2,1,0:T(8,128)(2,1)S(1)}, u32[]{:S(2)}, u32[]{:S(2)}) %collective-permute-start.14) | collective-permute-done | bytes 114720 | tf_op jit(solution)/shard_map/ppermute | solution.py:151
  64.8 0.1 pad_add_fusion.me
  64.9 2.8 %shard_map.118 = bf16[1024,128]{1,0:T(8,128)(2,1)} custom-call(s32[1]{0:T(128)} %bitcast.me, bf16[1024,128]{1,0:T(8,128)(2,1)S(1)} %bitcast.18, bf16[1024,128]{1,0:T(8,128)(2,1)S(1)} %collective-permute-done.before, bf16[1024,128]{1,0:T(8,128)(2,1)S(1)} %copy-done.6, bf16[27,128,128]{2,1,0:T(8,128)(2,1)S(1)} %bitcast.22), custom_call_target="tpu_custom_call" | custom-call | flops 905969664 | bytes 4194304 | tf_op jit(solution)/shard_map/pallas_call | solution.py:189
  67.7 1.7 %shard_map.124 = bf16[3456,128]{1,0:T(8,128)(2,1)} custom-call(s32[3]{0:T(128)S(1)} %pad_add_fusion.me, bf16[4,112,128]{2,1,0:T(8,128)(2,1)S(1)} %shard_map.123.refs_0_, bf16[4,112,128]{2,1,0:T(8,128)(2,1)S(1)} %collective-permute-done.12.refs_1_, bf16[4,112,128]{2,1,0:T(8,128)(2,1)S(1)} %collective-permute-done.13.refs_2_, ...), custom_call_target="tpu_custom_call" | custom-call | tf_op jit(solution)/shard_map/pallas_call | solution.py:206
  (29 shorter events, 0.2 us)
Async XLA Ops:
  0.6 19.2 %copy-start.4 = (bf16[1,1,64,16,128]{4,3,2,1,0:T(8,128)(2,1)S(1)}, bf16[1,1,64,16,128]{4,3,2,1,0:T(8,128)(2,1)}, u32[]{:S(2)}) copy-start(bf16[1,1,64,16,128]{4,3,2,1,0:T(8,128)(2,1)} %param.7) | copy-start | bytes 786436
  1.8 16.1 %collective-permute-start = (bf16[1024,128]{1,0:T(8,128)(2,1)S(1)}, bf16[1024,128]{1,0:T(8,128)(2,1)S(1)}, u32[]{:S(2)}, u32[]{:S(2)}) collective-permute-start(bf16[1024,128]{1,0:T(8,128)(2,1)S(1)} %bitcast.15), channel_id=1, source_target_pairs={{0,2},{2,4},{4,6},{6,8},{8,10},{10,12},{12,14},{14,16},{16,18},{18... | collective-permute-start | bytes 786440 | tf_op jit(solution)/shard_map/ppermute | solution.py:255
  6.7 13.1 %collective-permute-start.1 = (bf16[1024,128]{1,0:T(8,128)(2,1)S(1)}, bf16[1024,128]{1,0:T(8,128)(2,1)S(1)}, u32[]{:S(2)}, u32[]{:S(2)}) collective-permute-start(bf16[1024,128]{1,0:T(8,128)(2,1)S(1)} %bitcast.16), channel_id=1, source_target_pairs={{2,0},{4,2},{6,4},{8,6},{10,8},{12,10},{14,12},{16,14},{18,16},{20... | collective-permute-start | bytes 786440 | tf_op jit(solution)/shard_map/ppermute | solution.py:256
  19.8 1.9 %copy-start.5 = (bf16[1024,128]{1,0:T(8,128)(2,1)}, bf16[1024,128]{1,0:T(8,128)(2,1)S(1)}, u32[]{:S(2)}) copy-start(bf16[1024,128]{1,0:T(8,128)(2,1)S(1)} %collective-permute-done.1.after) | copy-start | bytes 786436
  21.7 2.5 %collective-permute-start.2 = (f32[16,112,128]{2,1,0:T(8,128)S(1)}, f32[16,112,128]{2,1,0:T(8,128)S(1)}, u32[]{:S(2)}, u32[]{:S(2)}) collective-permute-start(f32[16,112,128]{2,1,0:T(8,128)S(1)} %get-tuple-element.22), channel_id=1, source_target_pairs={{0,1},{1,0},{2,3},{3,2},{4,5},{5,4},{6,7},{7,6},{8,9},{9,8},{10,11... | collective-permute-start | bytes 2752520 | tf_op jit(solution)/shard_map/ppermute | solution.py:151
  24.2 40.7 %copy-start.3 = (bf16[3,3,3,128,128]{4,3,2,1,0:T(8,128)(2,1)S(1)}, bf16[3,3,3,128,128]{4,3,2,1,0:T(8,128)(2,1)}, u32[]{:S(2)}) copy-start(bf16[3,3,3,128,128]{4,3,2,1,0:T(8,128)(2,1)} %param.10) | copy-start | bytes 2654212
  25.1 8.7 %collective-permute-start.3 = (f32[4,112,128]{2,1,0:T(8,128)}, f32[4,112,128]{2,1,0:T(8,128)S(1)}, u32[]{:S(2)}, u32[]{:S(2)}) collective-permute-start(f32[4,112,128]{2,1,0:T(8,128)} %get-tuple-element.24), channel_id=1, source_target_pairs={{0,2},{2,0},{4,6},{6,4},{8,10},{10,8},{12,14},{14,12},{16,18},{18,... | collective-permute-start | bytes 688136 | tf_op jit(solution)/shard_map/ppermute | solution.py:151
  26.6 12.5 %collective-permute-start.4 = (f32[4,112,128]{2,1,0:T(8,128)}, f32[4,112,128]{2,1,0:T(8,128)S(1)}, u32[]{:S(2)}, u32[]{:S(2)}) collective-permute-start(f32[4,112,128]{2,1,0:T(8,128)} %get-tuple-element.25), channel_id=1, source_target_pairs={{0,4},{2,6},{4,0},{6,2},{8,12},{10,14},{12,8},{14,10},{16,20},{18,... | collective-permute-start | bytes 688136 | tf_op jit(solution)/shard_map/ppermute | solution.py:151
  26.6 12.5 %collective-permute-start.5 = (f32[4,112,128]{2,1,0:T(8,128)}, f32[4,112,128]{2,1,0:T(8,128)S(1)}, u32[]{:S(2)}, u32[]{:S(2)}) collective-permute-start(f32[4,112,128]{2,1,0:T(8,128)} %get-tuple-element.26), channel_id=1, source_target_pairs={{0,6},{2,4},{4,2},{6,0},{8,14},{10,12},{12,10},{14,8},{16,22},{18,... | collective-permute-start | bytes 688136 | tf_op jit(solution)/shard_map/ppermute | solution.py:151
  39.1 10.3 %copy-start = (f32[13824]{0:T(1024)S(1)}, f32[13824]{0:T(1024)}, u32[]{:S(2)}) copy-start(f32[13824]{0:T(1024)} %param.11) | copy-start | bytes 165892
  39.1 10.3 %copy-start.1 = (f32[13824]{0:T(1024)S(1)}, f32[13824]{0:T(1024)}, u32[]{:S(2)}) copy-start(f32[13824]{0:T(1024)} %param.12) | copy-start | bytes 165892
  39.1 10.3 %copy-start.2 = (f32[13824]{0:T(1024)S(1)}, f32[13824]{0:T(1024)}, u32[]{:S(2)}) copy-start(f32[13824]{0:T(1024)} %param.13) | copy-start | bytes 165892
  39.2 4.8 %collective-permute-start.6 = (f32[1,112,128]{2,1,0:T(8,128)S(1)}, f32[1,112,128]{2,1,0:T(8,128)S(1)}, u32[]{:S(2)}, u32[]{:S(2)}) collective-permute-start(f32[1,112,128]{2,1,0:T(8,128)S(1)} %get-tuple-element.28), channel_id=1, source_target_pairs={{0,8},{2,10},{4,12},{6,14},{8,0},{10,2},{12,4},{14,6},{16,24},{18,... | collective-permute-start | bytes 172040 | tf_op jit(solution)/shard_map/ppermute | solution.py:151
  40.8 6.3 %collective-permute-start.7 = (f32[1,112,128]{2,1,0:T(8,128)S(1)}, f32[1,112,128]{2,1,0:T(8,128)S(1)}, u32[]{:S(2)}, u32[]{:S(2)}) collective-permute-start(f32[1,112,128]{2,1,0:T(8,128)S(1)} %get-tuple-element.29), channel_id=1, source_target_pairs={{0,16},{2,18},{4,20},{6,22},{8,24},{10,26},{12,28},{14,30},{16,0},... | collective-permute-start | bytes 172040 | tf_op jit(solution)/shard_map/ppermute | solution.py:151
  43.4 6.0 %collective-permute-start.8 = (f32[1,112,128]{2,1,0:T(8,128)S(1)}, f32[1,112,128]{2,1,0:T(8,128)S(1)}, u32[]{:S(2)}, u32[]{:S(2)}) collective-permute-start(f32[1,112,128]{2,1,0:T(8,128)S(1)} %get-tuple-element.30), channel_id=1, source_target_pairs={{0,24},{2,26},{4,28},{6,30},{8,16},{10,18},{12,20},{14,22},{16,8},... | collective-permute-start | bytes 172040 | tf_op jit(solution)/shard_map/ppermute | solution.py:151
  49.4 15.5 %copy-start.6 = (bf16[1024,128]{1,0:T(8,128)(2,1)S(1)}, bf16[1024,128]{1,0:T(8,128)(2,1)}, u32[]{:S(2)}) copy-start(bf16[1024,128]{1,0:T(8,128)(2,1)} %copy-done.5) | copy-start | bytes 786436
  50.1 4.4 %collective-permute-start.9 = (bf16[1,112,128]{2,1,0:T(8,128)(2,1)S(1)}, bf16[1,112,128]{2,1,0:T(8,128)(2,1)S(1)}, u32[]{:S(2)}, u32[]{:S(2)}) collective-permute-start(bf16[1,112,128]{2,1,0:T(8,128)(2,1)S(1)} %get-tuple-element.35.refs_0_), channel_id=1, source_target_pairs={{0,8},{2,10},{4,12},{6,14},{8,0},{10,2},{12,4},{14,6},{16,24},{18,... | collective-permute-start | bytes 86024 | tf_op jit(solution)/shard_map/ppermute | solution.py:151
  50.1 4.8 %collective-permute-start.10 = (bf16[1,112,128]{2,1,0:T(8,128)(2,1)S(1)}, bf16[1,112,128]{2,1,0:T(8,128)(2,1)S(1)}, u32[]{:S(2)}, u32[]{:S(2)}) collective-permute-start(bf16[1,112,128]{2,1,0:T(8,128)(2,1)S(1)} %get-tuple-element.35.refs_0_), channel_id=1, source_target_pairs={{0,16},{2,18},{4,20},{6,22},{8,24},{10,26},{12,28},{14,30},{16,0},... | collective-permute-start | bytes 86024 | tf_op jit(solution)/shard_map/ppermute | solution.py:151
  51.4 5.7 %collective-permute-start.11 = (bf16[1,112,128]{2,1,0:T(8,128)(2,1)S(1)}, bf16[1,112,128]{2,1,0:T(8,128)(2,1)S(1)}, u32[]{:S(2)}, u32[]{:S(2)}) collective-permute-start(bf16[1,112,128]{2,1,0:T(8,128)(2,1)S(1)} %get-tuple-element.35.refs_0_), channel_id=1, source_target_pairs={{0,24},{2,26},{4,28},{6,30},{8,16},{10,18},{12,20},{14,22},{16,8},... | collective-permute-start | bytes 86024 | tf_op jit(solution)/shard_map/ppermute | solution.py:151
  57.1 4.9 %collective-permute-start.12 = (bf16[4,112,128]{2,1,0:T(8,128)(2,1)S(1)}, bf16[4,112,128]{2,1,0:T(8,128)(2,1)S(1)}, u32[]{:S(2)}, u32[]{:S(2)}) collective-permute-start(bf16[4,112,128]{2,1,0:T(8,128)(2,1)S(1)} %shard_map.123.refs_0_), channel_id=1, source_target_pairs={{0,2},{2,0},{4,6},{6,4},{8,10},{10,8},{12,14},{14,12},{16,18},{18,... | collective-permute-start | bytes 344072 | tf_op jit(solution)/shard_map/ppermute | solution.py:151
  57.7 4.8 %collective-permute-start.13 = (bf16[4,112,128]{2,1,0:T(8,128)(2,1)S(1)}, bf16[4,112,128]{2,1,0:T(8,128)(2,1)S(1)}, u32[]{:S(2)}, u32[]{:S(2)}) collective-permute-start(bf16[4,112,128]{2,1,0:T(8,128)(2,1)S(1)} %shard_map.123.refs_0_), channel_id=1, source_target_pairs={{0,4},{2,6},{4,0},{6,2},{8,12},{10,14},{12,8},{14,10},{16,20},{18,... | collective-permute-start | bytes 344072 | tf_op jit(solution)/shard_map/ppermute | solution.py:151
  59.1 5.7 %collective-permute-start.14 = (bf16[4,112,128]{2,1,0:T(8,128)(2,1)S(1)}, bf16[4,112,128]{2,1,0:T(8,128)(2,1)S(1)}, u32[]{:S(2)}, u32[]{:S(2)}) collective-permute-start(bf16[4,112,128]{2,1,0:T(8,128)(2,1)S(1)} %shard_map.123.refs_0_), channel_id=1, source_target_pairs={{0,6},{2,4},{4,2},{6,0},{8,14},{10,12},{12,10},{14,8},{16,22},{18,... | collective-permute-start | bytes 344072 | tf_op jit(solution)/shard_map/ppermute | solution.py:151
  60.6 7.1 %collective-permute-start.15 = (bf16[4,112,128]{2,1,0:T(8,128)(2,1)S(1)}, bf16[4,112,128]{2,1,0:T(8,128)(2,1)S(1)}, u32[]{:S(2)}, u32[]{:S(2)}) collective-permute-start(bf16[4,112,128]{2,1,0:T(8,128)(2,1)S(1)} %shard_map.123.refs_0_), channel_id=1, source_target_pairs={{0,1},{1,0},{2,3},{3,2},{4,5},{5,4},{6,7},{7,6},{8,9},{9,8},{10,11... | collective-permute-start | bytes 344072 | tf_op jit(solution)/shard_map/ppermute | solution.py:151
  61.9 5.8 %collective-permute-start.16 = (bf16[4,112,128]{2,1,0:T(8,128)(2,1)S(1)}, bf16[4,112,128]{2,1,0:T(8,128)(2,1)S(1)}, u32[]{:S(2)}, u32[]{:S(2)}) collective-permute-start(bf16[4,112,128]{2,1,0:T(8,128)(2,1)S(1)} %collective-permute-done.12.refs_1_), channel_id=1, source_target_pairs={{0,1},{1,0},{2,3},{3,2},{4,5},{5,4},{6,7},{7,6},{8,9},{9,8},{10,11... | collective-permute-start | bytes 344072 | tf_op jit(solution)/shard_map/ppermute | solution.py:151
  62.5 5.2 %collective-permute-start.17 = (bf16[4,112,128]{2,1,0:T(8,128)(2,1)S(1)}, bf16[4,112,128]{2,1,0:T(8,128)(2,1)S(1)}, u32[]{:S(2)}, u32[]{:S(2)}) collective-permute-start(bf16[4,112,128]{2,1,0:T(8,128)(2,1)S(1)} %collective-permute-done.13.refs_2_), channel_id=1, source_target_pairs={{0,1},{1,0},{2,3},{3,2},{4,5},{5,4},{6,7},{7,6},{8,9},{9,8},{10,11... | collective-permute-start | bytes 344072 | tf_op jit(solution)/shard_map/ppermute | solution.py:151
  64.8 2.9 %collective-permute-start.18 = (bf16[4,112,128]{2,1,0:T(8,128)(2,1)S(1)}, bf16[4,112,128]{2,1,0:T(8,128)(2,1)S(1)}, u32[]{:S(2)}, u32[]{:S(2)}) collective-permute-start(bf16[4,112,128]{2,1,0:T(8,128)(2,1)S(1)} %collective-permute-done.14.refs_3_), channel_id=1, source_target_pairs={{0,1},{1,0},{2,3},{3,2},{4,5},{5,4},{6,7},{7,6},{8,9},{9,8},{10,11... | collective-permute-start | bytes 344072 | tf_op jit(solution)/shard_map/ppermute | solution.py:151
